TPU v7x, 512 devices: a whole 4x4x16 slice. The times are simulated.
512 devices in a mesh: slab: 64 (over z, y), mem: 8 (over x, core).
Axes of the slice: x: 4, y: 4, z: 16, core: 2. Of those that a mesh axis runs over, the one named last changes fastest.
Arguments:
- present_ensemble: float32 [64, 4, 64, 512], P('mem', None, 'slab'), may hold values from -6 to 6
- delayed_ensemble: float32 [64, 2, 4, 64, 512], P('mem', None, None, 'slab'), may hold values from -6 to 6
- spreading_coefficient: float32 [64, 512], P('slab'), may hold values from 0.05 to 0.2
- transport_ratios: float32 [2, 64, 512], P(None, 'slab'), may hold values from -0.3 to 0.3
- obs_value: float32 [2, 256], replicated, may hold values from -6 to 6
- obs_error: float32 [2, 256], replicated, may hold values from 0.4 to 1.2
- obs_noise: float32 [2, 64, 256], replicated, may hold values from -6 to 6
- obs_row: int32 [2, 256], replicated, may hold values from 0 to 63
- obs_col: int32 [2, 256], replicated, may hold values from 1 to 510
- obs_field: int32 [2, 256], replicated, may hold values from 0 to 3
Outputs:
- analysis: float32 [64, 3, 4, 64, 512], P('mem', None, None, 'slab')
All inputs are finite; a program needn't handle non-finite values.
Results may differ from a plain program's by a relative error of at most 0.00011.
Values sent between devices are 32-bit elements; how exact they have to be, the bound alone decides.
A program may use at most 64 MiB of HBM per device.

v0:
```python
import jax
import jax.numpy as jnp
from jax import lax
from jax.sharding import PartitionSpec as P


def extended(shard, sides, width):
    for axis, dim in sides:
        devices, length = (lax.axis_size(axis), shard.shape[dim])
        up = [(i, (i + 1) % devices) for i in range(devices - 1)]
        down = [(j, i) for i, j in up]
        last = lax.slice_in_dim(shard, length - width, length, axis=dim)
        leading = lax.slice_in_dim(shard, 0, width, axis=dim)
        before = lax.ppermute(last, axis, up)
        after = lax.ppermute(leading, axis, down)
        shard = jnp.concatenate([before, shard, after], axis=dim)
    return shard


def propagate_ahead(present_ensemble, spreading_coefficient, transport_ratios):
    rowed = extended(present_ensemble, (("slab", 2),), 1)
    padded = jnp.pad(rowed, ((0, 0), (0, 0), (0, 0), (1, 1)))
    below = padded[:, :, 2:, 1:-1]
    above = padded[:, :, :-2, 1:-1]
    right = padded[:, :, 1:-1, 2:]
    left = padded[:, :, 1:-1, :-2]
    laplacian_operator = below + above + right + left - 4.0 * present_ensemble
    return (
        present_ensemble
        + spreading_coefficient * laplacian_operator
        - transport_ratios[0] * (below - above) * 0.5
        - transport_ratios[1] * (right - left) * 0.5
    )


def observe(level_zero, rows, cols, fields, row_start, col_start):
    members, nfield, height, width = level_zero.shape
    flat = level_zero.reshape(members, nfield * height * width)
    total = jnp.zeros((members, rows.shape[0]), jnp.float32)
    for offset, factor in ((-1, 0.25), (0, 0.5), (1, 0.25)):
        row_within = rows - row_start
        column_within = cols + offset - col_start
        valid = (
            (row_within >= 0)
            & (row_within < height)
            & (column_within >= 0)
            & (column_within < width)
        )
        index = (fields * height + jnp.clip(row_within, 0, height - 1)) * width + jnp.clip(
            column_within, 0, width - 1
        )
        picked = jnp.take(flat, index, axis=1)
        total = total + factor * jnp.where(valid[None, :], picked, 0.0)
    return total


def transform(observed, values, errors, noise):
    members = observed.shape[0]
    rescaled_values = (observed - jnp.mean(observed, axis=0, keepdims=True)) / errors[None, :]
    innovation = (values[None, :] - observed) / errors[None, :] + noise
    eye = jnp.eye(members, dtype=jnp.float32)
    system = (
        jnp.dot(
            rescaled_values,
            rescaled_values.T,
            precision=lax.Precision.HIGHEST,
            preferred_element_type=jnp.float32,
        )
        + (members - 1.0) * eye
    )
    right = jnp.dot(
        rescaled_values,
        innovation.T,
        precision=lax.Precision.HIGHEST,
        preferred_element_type=jnp.float32,
    )
    factor = jnp.linalg.cholesky(system)
    middle = lax.linalg.triangular_solve(factor, right, left_side=True, lower=True)
    weights = lax.linalg.triangular_solve(
        factor, middle, left_side=True, lower=True, transpose_a=True
    )
    return eye + weights - jnp.mean(weights, axis=0, keepdims=True)


def shards(
    present_ensemble,
    delayed_ensemble,
    spreading_coefficient,
    transport_ratios,
    obs_value,
    obs_error,
    obs_noise,
    obs_row,
    obs_col,
    obs_field,
):
    rows_here = present_ensemble.shape[2]
    row_start = lax.axis_index("slab") * rows_here
    predictive_dynamics = propagate_ahead(present_ensemble, spreading_coefficient, transport_ratios)
    flattened_system_array = jnp.concatenate(
        [predictive_dynamics[:, None], delayed_ensemble], axis=1
    )
    batch_count = obs_row.shape[0]
    columns = lax.all_to_all(flattened_system_array, "mem", split_axis=4, concat_axis=0, tiled=True)
    col_start = lax.axis_index("mem") * columns.shape[4]
    for batch in range(batch_count):
        partial_obs = observe(
            columns[:, 0], obs_row[batch], obs_col[batch], obs_field[batch], row_start, col_start
        )
        observed = lax.psum(partial_obs, ("slab", "mem"))
        matrix = transform(observed, obs_value[batch], obs_error[batch], obs_noise[batch])
        columns = jnp.einsum("jlfrn,jm->mlfrn", columns, matrix, precision=lax.Precision.HIGHEST)
    return lax.all_to_all(columns, "mem", split_axis=0, concat_axis=4, tiled=True)


def solution(mesh):
    return jax.shard_map(
        shards,
        mesh=mesh,
        in_specs=(
            P("mem", None, "slab", None),
            P("mem", None, None, "slab", None),
            P("slab", None),
            P(None, "slab", None),
            P(),
            P(),
            P(),
            P(),
            P(),
            P(),
        ),
        out_specs=P("mem", None, None, "slab", None),
        check_vma=False,
    )
```

profile of v0, /device:TPU:1, one launch (start us, length us, event | category | flops | bytes accessed | tf_op | source)
XLA Modules:
  0.0 1024.7 jit_solution(14442951278854169686)
XLA Ops:
  6.5 0.9 copy.140
  7.5 1.3 collective-permute-start
  8.8 4.7 collective-permute-start.1
  13.4 0.8 clamp_add_fusion.2
  14.2 0.8 clamp_add_fusion.1
  16.2 0.8 compare_and_fusion
  17.6 2.6 copy.142
  20.2 0.7 fusion.52
  20.9 1.5 fusion.51
  23.0 1.3 fusion.54
  24.3 1.3 fusion.53
  26.2 1.4 and_reduce_fusion.5
  27.8 1.3 copy.141
  29.2 2.7 fusion.57
  31.8 4.3 reshape.204
  36.1 10.0 all-to-all-start
  46.8 5.3 all-to-all-done
  52.6 1.0 reduce.16
  53.6 3.7 reshape.205
  57.3 1.5 copy.166
  59.0 0.7 gather_fusion.2
  59.7 0.7 gather_fusion.1
  60.4 0.9 gather_fusion
  61.4 1.6 fusion.11
  63.3 0.6 pad_clamp_fusion.2
  63.9 0.9 copy.170
  64.8 455.5 %all-reduce.4.cloned.1.call-done = f32[64,256]{0,1:T(8,128)} async-done(((f32[64,256]{0,1:T(8,128)}), f32[64,256]{0,1:T(8,128)}) %all-reduce.4.cloned.1.call-update) | async-done | bytes 65552 | tf_op jit(solution)/shard_map/psum | solution.py:110
  520.4 1.0 reduce_sum.36
  521.4 1.5 convolution_add_fusion.1
  523.1 5.8 cholesky.44
  528.9 0.6 compare_reduce_fusion.1
  529.6 0.7 fusion.29
  530.3 4.9 custom-call.11
  535.2 1.5 fusion.9
  537.9 0.7 gather_fusion.5
  538.6 0.7 gather_fusion.4
  539.3 0.7 gather_fusion.3
  540.1 0.9 fusion.5
  541.2 447.2 %all-reduce.6.cloned.1.call-done = f32[64,256]{0,1:T(8,128)} async-done(((f32[64,256]{0,1:T(8,128)}), f32[64,256]{0,1:T(8,128)}) %all-reduce.6.cloned.1.call-update) | async-done | bytes 65552 | tf_op jit(solution)/shard_map/psum | solution.py:110
  988.4 1.0 reduce_sum.38
  989.4 1.5 convolution_add_fusion
  991.1 5.8 cholesky.55
  997.6 0.7 fusion.30
  998.3 4.9 custom-call.13
  1003.2 1.5 fusion.3
  1006.4 9.0 all_to_all.36
  1015.4 1.0 reduce.17
  1017.0 0.9 all_to_all.33
  (78 shorter events, 8.9 us)
Async XLA Ops:
  6.5 21.2 %copy-start = (f32[8,4,1,512]{3,2,1,0:T(1,128)S(1)}, f32[8,4,1,512]{3,2,1,0:T(1,128)}, u32[]{:S(2)}) copy-start(f32[8,4,1,512]{3,2,1,0:T(1,128)} %param.17) | copy-start | bytes 196612
  6.5 21.2 %copy-start.2 = (f32[1,512]{1,0:T(1,128)S(1)}, f32[1,512]{1,0:T(1,128)}, u32[]{:S(2)}) copy-start(f32[1,512]{1,0:T(1,128)} %param.19) | copy-start | bytes 6148
  7.5 20.1 %collective-permute-start = (f32[8,4,1,512]{3,0,2,1:T(8,128)S(1)}, f32[8,4,1,512]{3,0,2,1:T(8,128)S(1)}, u32[]{:S(2)}, u32[]{:S(2)}) collective-permute-start(f32[8,4,1,512]{3,0,2,1:T(8,128)S(1)} %copy.140), channel_id=1, source_target_pairs={{8,0},{16,8},{24,16},{32,24},{40,32},{48,40},{56,48},{64,56},{72,6... | collective-permute-start | bytes 196616 | tf_op jit(solution)/shard_map/ppermute | solution.py:15
  8.8 18.8 %collective-permute-start.1 = (f32[8,4,1,512]{3,0,2,1:T(8,128)S(1)}, f32[8,4,1,512]{3,0,2,1:T(8,128)S(1)}, u32[]{:S(2)}, u32[]{:S(2)}) collective-permute-start(f32[8,4,1,512]{3,0,2,1:T(8,128)S(1)} %copy.140), channel_id=1, source_target_pairs={{0,8},{8,16},{16,24},{24,32},{32,40},{40,48},{48,56},{56,64},{64,7... | collective-permute-start | bytes 196616 | tf_op jit(solution)/shard_map/ppermute | solution.py:14
  36.1 15.9 %all-to-all-start = ((f32[8,1,6144]{2,1,0:T(1,128)}), f32[8,1,6144]{2,1,0:T(1,128)S(1)}, u32[]{:S(2)}, u32[]{:S(2)}) async-start(f32[8,1,6144]{2,1,0:T(1,128)} %reshape.204), calls=%async_computation | async-start | bytes 393216 | tf_op jit(solution)/shard_map/all_to_all | solution.py:104
  46.2 474.2 %all-reduce.4.cloned.1.call-start = ((), (), s32[]{:S(2)}) async-start(), calls=%async_computation.2 | async-start | bytes 262144 | tf_op jit(solution)/shard_map/psum | solution.py:110
  58.9 462.6 %copy-start.11 = (f32[1,256]{1,0:T(1,128)S(1)}, f32[1,256]{1,0:T(1,128)}, u32[]{:S(2)}) copy-start(f32[1,256]{1,0:T(1,128)} %get-tuple-element.33) | copy-start | bytes 3076
  58.9 476.3 %copy-start.10 = (f32[1,256]{1,0:T(1,128)S(1)}, f32[1,256]{1,0:T(1,128)}, u32[]{:S(2)}) copy-start(f32[1,256]{1,0:T(1,128)} %get-tuple-element.35) | copy-start | bytes 3076
  61.3 478.8 %copy-start.3 = (pred[256]{0:T(512)(128)(4,1)S(1)}, pred[256]{0:T(512)(128)(4,1)}, u32[]{:S(2)}) copy-start(pred[256]{0:T(512)(128)(4,1)} %get-tuple-element.46) | copy-start | bytes 772
  61.3 478.8 %copy-start.4 = (pred[256]{0:T(512)(128)(4,1)S(1)}, pred[256]{0:T(512)(128)(4,1)}, u32[]{:S(2)}) copy-start(pred[256]{0:T(512)(128)(4,1)} %get-tuple-element.47) | copy-start | bytes 772
  61.3 478.8 %copy-start.5 = (pred[256]{0:T(512)(128)(4,1)S(1)}, pred[256]{0:T(512)(128)(4,1)}, u32[]{:S(2)}) copy-start(pred[256]{0:T(512)(128)(4,1)} %get-tuple-element.6) | copy-start | bytes 772
  61.3 478.8 %copy-start.6 = (pred[256]{0:T(512)(128)(4,1)S(1)}, pred[256]{0:T(512)(128)(4,1)}, u32[]{:S(2)}) copy-start(pred[256]{0:T(512)(128)(4,1)} %get-tuple-element.8) | copy-start | bytes 772
  61.3 478.8 %copy-start.7 = (pred[256]{0:T(512)(128)(4,1)S(1)}, pred[256]{0:T(512)(128)(4,1)}, u32[]{:S(2)}) copy-start(pred[256]{0:T(512)(128)(4,1)} %get-tuple-element.10) | copy-start | bytes 772
  61.4 478.8 %copy-start.12 = (pred[256]{0:T(512)(128)(4,1)S(1)}, pred[256]{0:T(512)(128)(4,1)}, u32[]{:S(2)}) copy-start(pred[256]{0:T(512)(128)(4,1)} %compare_and_fusion.4) | copy-start | bytes 772
  63.0 478.1 %copy-start.1 = (f32[1,64,256]{2,1,0:T(8,128)S(1)}, f32[1,64,256]{2,1,0:T(8,128)}, u32[]{:S(2)}) copy-start(f32[1,64,256]{2,1,0:T(8,128)} %get-tuple-element.22) | copy-start | bytes 196612
  63.0 925.4 %all-reduce.6.cloned.1.call-start = ((), (), s32[]{:S(2)}) async-start(), calls=%async_computation.3 | async-start | bytes 262144 | tf_op jit(solution)/shard_map/psum | solution.py:110
  521.4 468.0 %copy-start.9 = (f32[1,256]{1,0:T(1,128)S(1)}, f32[1,256]{1,0:T(1,128)}, u32[]{:S(2)}) copy-start(f32[1,256]{1,0:T(1,128)} %get-tuple-element.32) | copy-start | bytes 3076
  530.2 472.9 %copy-start.8 = (f32[1,256]{1,0:T(1,128)S(1)}, f32[1,256]{1,0:T(1,128)}, u32[]{:S(2)}) copy-start(f32[1,256]{1,0:T(1,128)} %get-tuple-element.34) | copy-start | bytes 3076
Sparse Core Ops, SparseCore 0:
  63.1 457.1 all-reduce.3
  541.2 447.1 all-reduce.5
where the time goes:
time: 1030 us; the launch traced here: 1020 us
  waiting for transfers between devices  908 us (88%)
  other arithmetic  41.6 us (4%)
  local copies, waits for them, and re-layouts  27.9 us (3%)
  starting transfers between devices  16.2 us (2%)
  between operations  13.9 us (1%)
    psum x2, waiting for transfers between devices, shards(): observed = lax.psum(partial_obs, ('slab', 'mem'))  903 us
  transfers between devices with their start and end apart: 5, of which 3 were waited for; matrix products, arithmetic and copies ran while one was open for 2% of the time, Pallas kernels for 0%

commit v1 on v0

--- a/solution.py
+++ b/solution.py
@@ -107,7 +107,7 @@
         partial_obs = observe(
             columns[:, 0], obs_row[batch], obs_col[batch], obs_field[batch], row_start, col_start
         )
-        observed = lax.psum(partial_obs, ("slab", "mem"))
+        observed = jnp.sum(lax.all_gather(partial_obs, ("slab", "mem")), axis=0)
         matrix = transform(observed, obs_value[batch], obs_error[batch], obs_noise[batch])
         columns = jnp.einsum("jlfrn,jm->mlfrn", columns, matrix, precision=lax.Precision.HIGHEST)
     return lax.all_to_all(columns, "mem", split_axis=0, concat_axis=4, tiled=True)

time: 1030 us -> 637 us (0.62)
  waiting for transfers between devices: 908 us -> 473 us
  other arithmetic: 41.6 us -> 94.6 us
    psum x2 -> x0, waiting for transfers between devices: 903 us -> none  [shards(): observed = lax.psum(partial_obs, ('slab', 'mem'))]
    all_gather x0 -> x2, waiting for transfers between devices: none -> 468 us  [shards(): observed = jnp.sum(lax.all_gather(partial_obs, ('slab', 'mem')), axis=0)]
    reduce_sum x2, other arithmetic: 2.01 us -> 30 us  [transform(): jnp.mean(observed, axis=0, keepdims=True)]
    reduce_sum x0 -> x2, other arithmetic: none -> 25.9 us  [shards(): observed = jnp.sum(lax.all_gather(partial_obs, ('slab', 'mem')), axis=0)]
where the time goes in v1:
time: 637 us; the launch traced here: 636 us
  waiting for transfers between devices  473 us (74%)
  other arithmetic  94.6 us (15%)
  local copies, waits for them, and re-layouts  24.8 us (4%)
  starting transfers between devices  16.2 us (3%)
  between operations  13.8 us (2%)
  blocking collectives  10.2 us (2%)
    all_gather x2, waiting for transfers between devices, shards(): observed = jnp.sum(lax.all_gather(partial_obs, ('slab', 'mem')), axis=0)  468 us
    reduce_sum x2, other arithmetic, transform(): jnp.mean(observed, axis=0, keepdims=True)  30 us
    reduce_sum x2, other arithmetic, shards(): observed = jnp.sum(lax.all_gather(partial_obs, ('slab', 'mem')), axis=0)  25.9 us
    another operation x6, other arithmetic, transform(): factor = jnp.linalg.cholesky(system)  13 us
  transfers between devices with their start and end apart: 5, of which 3 were waited for; matrix products, arithmetic and copies ran while one was open for 2% of the time, Pallas kernels for 0%

profile of v1, /device:TPU:1, one launch (start us, length us, event | category | flops | bytes accessed | tf_op | source)
XLA Modules:
  0.0 635.5 jit_solution(16074655929105383639)
XLA Ops:
  6.5 0.9 copy.138
  7.4 1.3 collective-permute-start
  8.7 4.7 collective-permute-start.1
  13.4 1.4 clamp_add_fusion.2
  14.7 0.8 clamp_add_fusion.1
  15.5 0.6 compare_and_fusion.5
  16.1 0.8 compare_and_fusion
  16.9 0.7 fusion.53
  17.6 2.6 copy.140
  20.2 1.4 and_reduce_fusion.5
  22.3 1.0 subtract_bitcast_fusion
  23.3 1.3 copy.139
  24.6 2.7 fusion.58
  27.3 4.3 reshape.206
  31.6 10.0 %all-to-all-start = ((f32[8,1,6144]{2,1,0:T(1,128)}), f32[8,1,6144]{2,1,0:T(1,128)S(1)}, u32[]{:S(2)}, u32[]{:S(2)}) async-start(f32[8,1,6144]{2,1,0:T(1,128)} %reshape.206), calls=%async_computation | async-start | bytes 393216 | tf_op jit(solution)/shard_map/all_to_all | solution.py:104
  42.2 5.3 all-to-all-done
  48.0 1.0 reduce.20
  49.0 3.7 reshape.207
  52.8 1.5 copy.164
  54.4 0.7 gather_fusion.1
  55.1 0.7 gather_fusion.2
  55.9 0.9 gather_fusion
  56.7 1.0 fusion.9
  57.7 0.7 copy.144
  58.7 0.7 compare_select_fusion.2
  59.4 0.7 compare_and_fusion.4
  60.1 0.8 fusion.54
  60.9 235.9 %all-gather.5.cloned.1.call-done = f32[32768,256]{1,0:T(8,128)} async-done(((f32[64,256]{1,0:T(8,128)}), f32[32768,256]{1,0:T(8,128)}) %all-gather.5.cloned.1.call-update) | async-done | bytes 33554448 | tf_op jit(solution)/shard_map/all_gather | solution.py:110
  296.8 12.9 %reduce_sum.54 = f32[64,256]{1,0:T(8,128)S(1)} reduce(f32[512,64,256]{2,1,0:T(8,128)} %bitcast.137, f32[]{:T(128)} %constant.76.clone.1), dimensions={0}, to_apply=%region_0.2 | reduce | flops 8372224 | bytes 33619972 | tf_op jit(solution)/shard_map/reduce_sum | solution.py:110
  309.7 15.0 %reduce_sum.55 = f32[256]{0:T(256)S(1)} reduce(f32[32768,256]{1,0:T(8,128)} %all-gather.5.cloned.1.call-done, f32[]{:T(128)} %constant.76.clone.1), dimensions={0}, to_apply=%region_1.3 | reduce | flops 8388352 | bytes 33555460 | tf_op jit(solution)/shard_map/reduce_sum | solution.py:59
  325.1 5.8 cholesky.44
  331.0 0.6 compare_reduce_fusion.1
  331.6 0.7 fusion.21
  332.3 4.9 custom-call.11
  338.6 0.7 gather_fusion.4
  339.3 0.7 gather_fusion.3
  340.1 0.7 gather_fusion.5
  341.1 0.7 copy.153
  341.8 232.0 %all-gather.7.cloned.1.call-done = f32[32768,256]{1,0:T(8,128)} async-done(((f32[64,256]{1,0:T(8,128)}), f32[32768,256]{1,0:T(8,128)}) %all-gather.7.cloned.1.call-update) | async-done | bytes 33554448 | tf_op jit(solution)/shard_map/all_gather | solution.py:110
  573.8 12.9 %reduce_sum.57 = f32[64,256]{1,0:T(8,128)S(1)} reduce(f32[512,64,256]{2,1,0:T(8,128)} %bitcast.138, f32[]{:T(128)} %constant.76.clone.1), dimensions={0}, to_apply=%region_5.10 | reduce | flops 8372224 | bytes 33619972 | tf_op jit(solution)/shard_map/reduce_sum | solution.py:110
  586.8 15.0 %reduce_sum.58 = f32[256]{0:T(256)S(1)} reduce(f32[32768,256]{1,0:T(8,128)} %all-gather.7.cloned.1.call-done, f32[]{:T(128)} %constant.76.clone.1), dimensions={0}, to_apply=%region_6.11 | reduce | flops 8388352 | bytes 33555460 | tf_op jit(solution)/shard_map/reduce_sum | solution.py:59
  602.1 5.8 cholesky.55
  608.0 0.6 compare_reduce_fusion
  608.6 0.7 fusion.22
  609.3 4.9 custom-call.13
  616.1 10.2 %all_to_all.36 = f32[8,1,6144]{2,1,0:T(1,128)S(1)} all-to-all(f32[8,1,6144]{2,1,0:T(1,128)S(1)} %reshape.208), channel_id=1, replica_groups=mesh['slab'=64,'mem'=8] {'mem'}, dimensions={0} | all-to-all | bytes 393216 | tf_op jit(solution)/shard_map/all_to_all | solution.py:113
  626.2 1.0 reduce.21
  627.8 0.9 all_to_all.33
  (63 shorter events, 6.9 us)
Async XLA Ops:
  7.4 14.8 %collective-permute-start = (f32[8,4,1,512]{3,0,2,1:T(8,128)S(1)}, f32[8,4,1,512]{3,0,2,1:T(8,128)S(1)}, u32[]{:S(2)}, u32[]{:S(2)}) collective-permute-start(f32[8,4,1,512]{3,0,2,1:T(8,128)S(1)} %copy.138), channel_id=1, source_target_pairs={{8,0},{16,8},{24,16},{32,24},{40,32},{48,40},{56,48},{64,56},{72,6... | collective-permute-start | bytes 196616 | tf_op jit(solution)/shard_map/ppermute | solution.py:15
  8.7 13.5 %collective-permute-start.1 = (f32[8,4,1,512]{3,0,2,1:T(8,128)S(1)}, f32[8,4,1,512]{3,0,2,1:T(8,128)S(1)}, u32[]{:S(2)}, u32[]{:S(2)}) collective-permute-start(f32[8,4,1,512]{3,0,2,1:T(8,128)S(1)} %copy.138), channel_id=1, source_target_pairs={{0,8},{8,16},{16,24},{24,32},{32,40},{40,48},{48,56},{56,64},{64,7... | collective-permute-start | bytes 196616 | tf_op jit(solution)/shard_map/ppermute | solution.py:14
  31.6 15.9 %all-to-all-start = ((f32[8,1,6144]{2,1,0:T(1,128)}), f32[8,1,6144]{2,1,0:T(1,128)S(1)}, u32[]{:S(2)}, u32[]{:S(2)}) async-start(f32[8,1,6144]{2,1,0:T(1,128)} %reshape.206), calls=%async_computation | async-start | bytes 393216 | tf_op jit(solution)/shard_map/all_to_all | solution.py:104
  41.6 255.2 %all-gather.5.cloned.1.call-start = ((), (), s32[]{:S(2)}) async-start(), calls=%async_computation.2 | async-start | bytes 33619968 | tf_op jit(solution)/shard_map/all_gather | solution.py:110
  54.3 6.6 %copy-start = (f32[2,256]{1,0:T(2,128)S(1)}, f32[2,256]{1,0:T(2,128)}, u32[]{:S(2)}) copy-start(f32[2,256]{1,0:T(2,128)} %param.21) | copy-start | bytes 6148
  58.5 515.4 %all-gather.7.cloned.1.call-start = ((), (), s32[]{:S(2)}) async-start(), calls=%async_computation.3 | async-start | bytes 33619968 | tf_op jit(solution)/shard_map/all_gather | solution.py:110
  309.7 27.5 %copy-start.4 = (f32[2,64,256]{2,1,0:T(8,128)S(1)}, f32[2,64,256]{2,1,0:T(8,128)}, u32[]{:S(2)}) copy-start(f32[2,64,256]{2,1,0:T(8,128)} %param.23) | copy-start | bytes 393220
  324.8 16.0 %copy-start.1 = (pred[256]{0:T(512)(128)(4,1)S(1)}, pred[256]{0:T(512)(128)(4,1)}, u32[]{:S(2)}) copy-start(pred[256]{0:T(512)(128)(4,1)} %get-tuple-element.6) | copy-start | bytes 772
  324.8 16.0 %copy-start.2 = (pred[256]{0:T(512)(128)(4,1)S(1)}, pred[256]{0:T(512)(128)(4,1)}, u32[]{:S(2)}) copy-start(pred[256]{0:T(512)(128)(4,1)} %get-tuple-element.8) | copy-start | bytes 772
  324.8 16.0 %copy-start.3 = (pred[256]{0:T(512)(128)(4,1)S(1)}, pred[256]{0:T(512)(128)(4,1)}, u32[]{:S(2)}) copy-start(pred[256]{0:T(512)(128)(4,1)} %get-tuple-element.10) | copy-start | bytes 772
Sparse Core Ops, SparseCore 0:
  58.6 238.1 all-gather.4
  341.9 231.8 all-gather.6
